TPU v7x, 32 devices: a whole 2x2x4 slice. The times are simulated.
32 devices in a mesh: groups: 2 (over x), ctx: 16 (over z, y, core).
Axes of the slice: x: 2, y: 2, z: 4, core: 2. Of those that a mesh axis runs over, the one named last changes fastest.
Arguments:
- queries: bfloat16 [12288, 1024], P(('groups', 'ctx')), parts along dimension 0
- keys: bfloat16 [12288, 1024], P(('groups', 'ctx')), parts along dimension 0
- values: bfloat16 [12288, 1024], P(('groups', 'ctx')), parts along dimension 0, may hold values from -6 to 6
- out_weight: bfloat16 [1024, 1024], P('ctx'), may hold values from -0.1875 to 0.1875
- grad_output: bfloat16 [12288, 1024], P(('groups', 'ctx')), parts along dimension 0, may hold values from -6 to 6
- complex_id: int32 [12288], P('groups'), parts along dimension 0, may hold values from 0 to 3, never falling along the last dimension, each value on 1 to 3072 neighbouring positions
- contacts: int32 [96, 6], P(('groups', 'ctx')), parts along dimension 0, may hold values from 0 to 47, as said below
- contact_count: int32 [96], P(('groups', 'ctx')), parts along dimension 0, may hold values from 3 to 6, as said below
Outputs:
- mixed: bfloat16 [12288, 1024], P(('groups', 'ctx')), parts along dimension 0
- grad_queries: bfloat16 [12288, 1024], P(('groups', 'ctx')), parts along dimension 0
- grad_keys: bfloat16 [12288, 1024], P(('groups', 'ctx')), parts along dimension 0
- grad_values: bfloat16 [12288, 1024], P(('groups', 'ctx')), parts along dimension 0
- grad_weight: float32 [2048, 1024], P(('groups', 'ctx')), parts along dimension 0
There are 2 independent parts, one for each index of `groups`. A program takes and returns all parts, laid end to end along the dimension named above; an argument that names none is the same for every part. Nothing has to cross between parts.
Inputs may be any that keep to these rules, and one draw needn't show every extreme that they name: `contacts`: entry 0 of each list is the query block itself; the other entries are distinct blocks, other than the query block, at most 6 blocks from it. `contact_count`: on some device every block of the device has all 6 entries live.
All inputs are finite; a program needn't handle non-finite values.
Results may differ from a plain program's by a relative error of at most 0.022.
Values may be sent and summed in bfloat16 or wider, within the bound.
A program may use at most 192 MiB of HBM per device.

v0:
```python
import functools
import math

import jax
import jax.numpy as jnp
from jax import lax
from jax.experimental import pallas as pl
from jax.experimental.pallas import tpu as pltpu
from jax.sharding import PartitionSpec as P

HEADS = 16
REACH_DEV = 2
LANES = 128


def neighbours(n):
    me = lax.axis_index("ctx")
    core, y = lax.rem(me, 2), lax.rem(me // 2, 2)
    ahead, behind = me + 4 - 8 * y, me - 4 + 8 * y
    has_ahead = (ahead >= 0) & (ahead < n)
    has_behind = (behind >= 0) & (behind < n)
    return core, y, me + 2 - 4 * y, me + 1 - 2 * core, ahead, behind, has_ahead, has_behind


def greet(ypeer, cpeer, ahead, behind, has_ahead, has_behind):
    barrier = pltpu.get_barrier_semaphore()

    def hello(device):
        pl.semaphore_signal(barrier, inc=1, device_id={"ctx": device}, device_id_type=pl.DeviceIdType.MESH)

    hello(ypeer)
    hello(cpeer)
    pl.when(has_ahead)(lambda: hello(ahead))
    pl.when(has_behind)(lambda: hello(behind))
    pl.semaphore_wait(barrier, 2 + has_ahead.astype(jnp.int32) + has_behind.astype(jnp.int32))


def remote(src, dst, send, recv, device):
    return pltpu.make_async_remote_copy(
        src_ref=src, dst_ref=dst, send_sem=send, recv_sem=recv,
        device_id={"ctx": device}, device_id_type=pl.DeviceIdType.MESH,
    )


def gather_kernel(n, chunks, k_ref, v_ref, kwin, vwin, sends, recvs):
    core, y, ypeer, cpeer, ahead, behind, has_ahead, has_behind = neighbours(n)
    greet(ypeer, cpeer, ahead, behind, has_ahead, has_behind)
    step = k_ref.shape[0] // chunks
    owns, wins = (k_ref, v_ref), (kwin, vwin)
    total = 2 * chunks

    def at(c):
        return c % 2, pl.ds((c // 2) * step, step)

    def over_y(c):
        a, r = at(c)
        return remote(owns[a].at[r], wins[a].at[3 * y, r], sends.at[0, c], recvs.at[0, c], ypeer)

    def over_z(c):
        a, r = at(c)
        return remote(wins[a].at[3 - 3 * y, r], wins[a].at[3 * y, r], sends.at[1, c], recvs.at[1, c], ahead)

    def across(c):
        a, r = at(c)
        return remote(owns[a].at[r], wins[a].at[1 + core, r], sends.at[2, c], recvs.at[2, c], cpeer)

    def onward(c):
        a, r = at(c)
        return remote(
            wins[a].at[3 - 3 * core, r], wins[a].at[2 - core, r], sends.at[3, c], recvs.at[3, c], cpeer
        )

    def late(c):
        pl.when(has_behind)(lambda: over_z(c).wait_recv())
        pl.when(has_behind & (y != core))(lambda: onward(c).start())

    for c in range(total):
        over_y(c).start()
    for c in range(total):
        across(c).start()
    for c in range(total):
        over_y(c).wait_recv()
        pl.when(has_ahead)(lambda c=c: over_z(c).start())
        pl.when(y == core)(lambda c=c: onward(c).start())
        if c:
            late(c - 1)
    late(total - 1)
    for c in range(total):
        over_y(c).wait_send()
        pl.when(has_ahead)(lambda c=c: over_z(c).wait_send())
        across(c).wait_send()
        across(c).wait_recv()
        pl.when((y == core) | has_behind)(lambda c=c: onward(c).wait_send())
        pl.when((y != core) | has_behind)(lambda c=c: onward(c).wait_recv())


def gather_window(keys, values, chunks=6):
    n = lax.axis_size("ctx")
    any_space = pl.BlockSpec(memory_space=pl.ANY)
    shape = jax.ShapeDtypeStruct((2 * REACH_DEV,) + keys.shape, keys.dtype)
    return pl.pallas_call(
        functools.partial(gather_kernel, n, chunks),
        out_shape=[shape, shape],
        in_specs=[any_space] * 2,
        out_specs=[any_space] * 2,
        scratch_shapes=[pltpu.SemaphoreType.DMA((4, 2 * chunks)), pltpu.SemaphoreType.DMA((4, 2 * chunks))],
        compiler_params=pltpu.CompilerParams(collective_id=0, has_side_effects=True),
        cost_estimate=pl.CostEstimate(flops=0, bytes_accessed=150_000_000, transcendentals=0),
        name="gather_window",
    )(keys, values)


def return_kernel(n, chunks, far, own, gk_ref, gv_ref, got_f, got_c, got_z, got_y, put_z, put_y, sends, recvs):
    core, y, ypeer, cpeer, ahead, behind, has_ahead, has_behind = neighbours(n)
    greet(ypeer, cpeer, ahead, behind, has_ahead, has_behind)
    step = own.shape[1] // chunks
    total = 2 * chunks
    f32, bf16 = jnp.float32, jnp.bfloat16

    def at(c):
        return c % 2, pl.ds((c // 2) * step, step)

    def back(c):
        a, r = at(c)
        return remote(far.at[1 + core, a, r], got_f.at[a, r], sends.at[0, c], recvs.at[0, c], cpeer)

    def across(c):
        a, r = at(c)
        return remote(far.at[2 - core, a, r], got_c.at[a, r], sends.at[1, c], recvs.at[1, c], cpeer)

    def over_z(c):
        a, r = at(c)
        return remote(put_z.at[a, r], got_z.at[a, r], sends.at[2, c], recvs.at[2, c], behind)

    def over_y(c):
        a, r = at(c)
        return remote(put_y.at[a, r], got_y.at[a, r], sends.at[3, c], recvs.at[3, c], ypeer)

    sent_back = (y != core) | has_behind
    got_back = (y == core) | has_behind
    for c in range(total):
        pl.when(sent_back)(lambda c=c: back(c).start())

    def second(c):
        a, r = at(c)
        pl.when(has_ahead)(lambda: over_z(c).wait_recv())
        value = far[3 - 3 * y, a, r, :].astype(f32)
        value = value + jnp.where(has_ahead, got_z[a, r, :].astype(f32), 0.0)
        value = value + jnp.where(y == core, got_f[a, r, :].astype(f32), 0.0)
        put_y[a, r, :] = value.astype(bf16)
        over_y(c).start()

    for c in range(total):
        a, r = at(c)
        pl.when(got_back)(lambda c=c: back(c).wait_recv())
        value = far[3 * y, a, r, :].astype(f32)
        put_z[a, r, :] = (value + jnp.where(y != core, got_f[a, r, :].astype(f32), 0.0)).astype(bf16)
        pl.when(has_behind)(lambda c=c: over_z(c).start())
        across(c).start()
        if c >= 2:
            second(c - 2)
    second(total - 2)
    second(total - 1)
    for c in range(total):
        a, r = at(c)
        across(c).wait_recv()
        over_y(c).wait_recv()
        value = own[a, r, :] + got_c[a, r, :].astype(f32) + got_y[a, r, :].astype(f32)
        (gk_ref, gv_ref)[a][r, :] = value.astype(bf16)
    for c in range(total):
        pl.when(sent_back)(lambda c=c: back(c).wait_send())
        across(c).wait_send()
        pl.when(has_behind)(lambda c=c: over_z(c).wait_send())
        over_y(c).wait_send()


def return_grads(far, own, chunks=6):
    n = lax.axis_size("ctx")
    _, rows, width = own.shape
    space = pl.BlockSpec(memory_space=pltpu.VMEM)
    shape = jax.ShapeDtypeStruct((rows, width), jnp.bfloat16)
    return pl.pallas_call(
        functools.partial(return_kernel, n, chunks),
        out_shape=[shape, shape],
        in_specs=[space] * 2,
        out_specs=[space] * 2,
        scratch_shapes=[pltpu.VMEM((2, rows, width), jnp.bfloat16)] * 6
        + [pltpu.SemaphoreType.DMA((4, 2 * chunks)), pltpu.SemaphoreType.DMA((4, 2 * chunks))],
        compiler_params=pltpu.CompilerParams(
            collective_id=1, has_side_effects=True, vmem_limit_bytes=56 * 1024 * 1024
        ),
        cost_estimate=pl.CostEstimate(flops=0, bytes_accessed=150_000_000, transcendentals=0),
        name="return_grads",
    )(far, own)


def attention_kernel(
    blocks, listed, block, head_dim,
    local_ref, count_ref, q_ref, k_ref, v_ref, d_ref,
    kfar, vfar, idk_ref, idq_ref,
    att_ref, dq_ref, own_ref, far_ref,
    kwin, vwin, bias, gk, gv, kg, vg,
):
    rows = blocks * block
    scale = 1.0 / math.sqrt(head_dim)
    f32, bf16 = jnp.float32, jnp.bfloat16

    @pl.when(pl.program_id(0) == 0)
    def _():
        for b in range(blocks):
            mine = idq_ref[b : b + 1, :]
            for j in range(listed):
                start = pl.multiple_of(local_ref[b, j] * block, block)
                same = idk_ref[pl.ds(start, block), :] == mine
                alive = jnp.where(j < count_ref[b], 0.0, -jnp.inf).astype(f32)
                bias[pl.ds((b * listed + j) * block, block), :] = jnp.where(same, alive, -jnp.inf)

    for i, piece in enumerate((0, 1, None, 2, 3)):
        span = pl.ds(i * rows, rows)
        kwin[span, :] = k_ref[...] if piece is None else kfar[piece]
        vwin[span, :] = v_ref[...] if piece is None else vfar[piece]
    gk[...] = jnp.zeros_like(gk)
    gv[...] = jnp.zeros_like(gv)

    lane = lax.broadcasted_iota(jnp.int32, (block, LANES), 1) < head_dim
    sub = lax.broadcasted_iota(jnp.int32, (LANES, block), 0) < head_dim
    last = (((1,), (1,)), ((), ()))
    first = (((0,), (0,)), ((), ()))

    def two(x):
        zero = jnp.zeros_like(x)
        return jnp.concatenate([jnp.where(lane, x, zero), jnp.where(lane, zero, x)], axis=0).astype(bf16)

    for b in range(blocks):
        here = pl.ds(b * block, block)
        starts = [pl.multiple_of(local_ref[b, j] * block, block) for j in range(listed)]
        for j in range(listed):
            kg[pl.ds(j * block, block), :] = kwin[pl.ds(starts[j], block), :]
            vg[pl.ds(j * block, block), :] = vwin[pl.ds(starts[j], block), :]
        grad = d_ref[here, :].astype(f32)
        q2 = two(q_ref[here, :].astype(f32) * scale)
        d2 = two(grad)
        s = lax.dot_general(kg[...], q2, last, preferred_element_type=f32)
        mask = bias[pl.ds(b * listed * block, listed * block), :]
        s = s + jnp.concatenate([mask, mask], axis=1)
        top = jnp.max(s, axis=0, keepdims=True)
        e = jnp.exp(s - top)
        probs = e * (1.0 / jnp.sum(e, axis=0, keepdims=True))
        low = probs.astype(bf16)
        ot = lax.dot_general(vg[...], low, first, preferred_element_type=f32)
        att = jnp.where(sub, ot[:, :block], ot[:, block:]).astype(bf16).astype(f32)
        att_ref[here, :] = att.T.astype(bf16)
        prod = grad.T * att
        row_dot = jnp.concatenate(
            [jnp.sum(prod[:head_dim], axis=0, keepdims=True), jnp.sum(prod[head_dim:], axis=0, keepdims=True)],
            axis=1,
        )
        dp = lax.dot_general(vg[...], d2, last, preferred_element_type=f32)
        ds = (probs * (dp - row_dot)).astype(bf16)
        dqt = lax.dot_general(kg[...], ds, first, preferred_element_type=f32)
        dq = jnp.where(sub, dqt[:, :block], dqt[:, block:]) * scale
        dq_ref[here, :] = dq.T.astype(bf16)
        dk = jnp.dot(ds, q2, preferred_element_type=f32)
        dv = jnp.dot(low, d2, preferred_element_type=f32)
        for j in range(listed):
            part = slice(j * block, (j + 1) * block)
            gk[pl.ds(starts[j], block), :] += dk[part]
            gv[pl.ds(starts[j], block), :] += dv[part]

    own = pl.ds(REACH_DEV * rows, rows)
    own_ref[0] = gk[own, :]
    own_ref[1] = gv[own, :]
    for i, at in enumerate((0, 1, 3, 4)):
        span = pl.ds(at * rows, rows)
        far_ref[i, 0] = gk[span, :].astype(bf16)
        far_ref[i, 1] = gv[span, :].astype(bf16)


def attention(local, count, queries, keys, values, grad_input, kfar, vfar, idk, idq):
    rows, width = queries.shape
    blocks, listed = local.shape
    block = rows // blocks
    head_dim = width // HEADS
    window = (2 * REACH_DEV + 1) * rows
    flat = pl.BlockSpec((rows, LANES), lambda p, *_: (0, p))
    pair = pl.BlockSpec((2, rows, LANES), lambda p, *_: (0, 0, p))
    quad = pl.BlockSpec((2 * REACH_DEV, rows, LANES), lambda p, *_: (0, 0, p))
    far = pl.BlockSpec((2 * REACH_DEV, 2, rows, LANES), lambda p, *_: (0, 0, 0, p))
    whole = lambda shape: pl.BlockSpec(shape, lambda p, *_: (0, 0))
    f32, bf16 = jnp.float32, jnp.bfloat16
    return pl.pallas_call(
        functools.partial(attention_kernel, blocks, listed, block, head_dim),
        grid_spec=pltpu.PrefetchScalarGridSpec(
            num_scalar_prefetch=2,
            grid=(width // LANES,),
            in_specs=[flat, flat, flat, flat, quad, quad, whole(idk.shape), whole(idq.shape)],
            out_specs=[flat, flat, pair, far],
            scratch_shapes=[
                pltpu.VMEM((window, LANES), bf16),
                pltpu.VMEM((window, LANES), bf16),
                pltpu.VMEM((blocks * listed * block, LANES), f32),
                pltpu.VMEM((window, LANES), f32),
                pltpu.VMEM((window, LANES), f32),
                pltpu.VMEM((listed * block, LANES), bf16),
                pltpu.VMEM((listed * block, LANES), bf16),
            ],
        ),
        out_shape=[
            jax.ShapeDtypeStruct((rows, width), bf16),
            jax.ShapeDtypeStruct((rows, width), bf16),
            jax.ShapeDtypeStruct((2, rows, width), f32),
            jax.ShapeDtypeStruct((2 * REACH_DEV, 2, rows, width), bf16),
        ],
        compiler_params=pltpu.CompilerParams(dimension_semantics=("arbitrary",)),
        name="contact_attention",
    )(local, count, queries, keys, values, grad_input, kfar, vfar, idk, idq)


def shards(queries, keys, values, out_weight, grad_output, complex_id, contacts, contact_count):
    rows, width = queries.shape
    local_blocks, listed = contacts.shape
    block = rows // local_blocks
    position = lax.axis_index("ctx")
    total_tokens = rows * lax.axis_size("ctx")
    f32, bf16 = jnp.float32, jnp.bfloat16
    weight = lax.all_gather(out_weight, "ctx", axis=0, tiled=True)
    kfar, vfar = gather_window(keys, values)
    grad_input = lax.dot_general(
        grad_output, weight, (((1,), (1,)), ((), ())), preferred_element_type=f32
    ).astype(bf16)
    margin = REACH_DEV * rows
    ids = lax.dynamic_slice_in_dim(
        jnp.pad(complex_id, (margin, margin), constant_values=-1), position * rows, rows + 2 * margin
    )
    idk = jnp.broadcast_to(ids[:, None], (rows + 2 * margin, LANES))
    idq = ids[margin : margin + rows].reshape(local_blocks, block)
    local = contacts - (position - REACH_DEV) * local_blocks
    attended, grad_queries, own, far = attention(
        local, contact_count, queries, keys, values, grad_input,
        kfar, vfar, idk, idq,
    )
    grad_keys, grad_values = return_grads(far, own)
    mixed = jnp.dot(attended, weight, preferred_element_type=f32).astype(bf16)
    grad_weight = lax.psum_scatter(
        lax.dot_general(attended, grad_output, (((0,), (0,)), ((), ())), preferred_element_type=f32).astype(bf16),
        "ctx",
        scatter_dimension=0,
        tiled=True,
    ).astype(f32) * jnp.float32(1.0 / math.sqrt(total_tokens))
    return mixed, grad_queries, grad_keys, grad_values, grad_weight


def solution(mesh):
    split = P(("groups", "ctx"), None)
    return jax.shard_map(
        shards,
        mesh=mesh,
        in_specs=(split, split, split, P("ctx", None), split, P("groups"), split, P(("groups", "ctx"))),
        out_specs=(split,) * 5,
        check_vma=False,
    )
```

profile of v0, /device:TPU:22, one launch (start us, length us, event | category | flops | bytes accessed | tf_op | source)
XLA Modules:
  0.0 190.6 jit_solution(12227510440370093366)
XLA Ops:
  7.2 0.0 copy-start
  7.2 0.0 all-gather.2.cloned.1.call-start
  7.2 0.7 all-gather.2.cloned.1.call-update
  7.9 0.0 reduce-scatter.2.cloned.1.call-start
  8.0 57.2 %gather_window.1 = (bf16[4,384,1024]{2,1,0:T(8,128)(2,1)}, bf16[4,384,1024]{2,1,0:T(8,128)(2,1)}) custom-call(bf16[384,1024]{1,0:T(8,128)(2,1)} %k_ref.3, bf16[384,1024]{1,0:T(8,128)(2,1)} %v_ref.3), custom_call_target="tpu_custom_call" | custom-call | bytes 150000000 | tf_op jit(solution)/shard_map/gather_window/pallas_call | solution.py:101
  65.2 1.4 fusion.idq_ref
  66.6 0.8 pad_dynamic-slice_fusion.1
  67.4 1.3 broadcast_subtract_fusion.local_ref
  68.6 0.0 all-gather.2.cloned.1.call-done
  68.6 0.0 copy-done
  68.6 3.5 %convolution_convert_fusion.2.d_ref = bf16[384,1024]{1,0:T(8,128)(2,1)} fusion(bf16[384,1024]{1,0:T(8,128)(2,1)S(1)} %copy-done, bf16[1024,1024]{1,0:T(8,128)(2,1)} %all-gather.2.cloned.1.call-done), kind=kOutput, calls=%fused_computation.2 | convolution fusion | flops 805699584 | bytes 3670016 | tf_op jit(solution)/shard_map/dot_general | solution.py:328
  72.1 1.3 broadcast_in_dim.2.idk_ref
  73.4 35.7 %contact_attention.1 = (bf16[384,1024]{1,0:T(8,128)(2,1)}, bf16[384,1024]{1,0:T(8,128)(2,1)}, f32[2,384,1024]{2,1,0:T(8,128)}, bf16[4,2,384,1024]{3,2,1,0:T(8,128)(2,1)}) custom-call(s32[3,6]{1,0:T(4,128)} %broadcast_subtract_fusion.local_ref, s32[3]{0:T(128)} %count_ref.1, bf16[384,1024]{1,0:T(8,128)(2,1)} %q_ref.1, bf16[384,1024]{1,0:T(8,128)(2,1)} %k_ref.3, ...), custom_call_target="tpu_custom_call" | custom-call | tf_op jit(solution)/shard_map/contact_attention/pallas_call | solution.py:291
  109.2 3.7 %convolution_convert_fusion = bf16[1024,1024]{1,0:T(8,128)(2,1)} fusion(bf16[384,1024]{1,0:T(8,128)(2,1)} %get-tuple-element.15, bf16[384,1024]{1,0:T(8,128)(2,1)S(1)} %copy-done), kind=kOutput, calls=%fused_computation | convolution fusion | flops 806354944 | bytes 3670016 | tf_op jit(solution)/shard_map/dot_general | solution.py:345
  112.9 0.0 reduce-scatter.2.cloned.1.call-update
  112.9 0.0 copy-start.3
  112.9 0.0 copy-start.4
  112.9 55.6 %return_grads.1 = (bf16[384,1024]{1,0:T(8,128)(2,1)}, bf16[384,1024]{1,0:T(8,128)(2,1)}) custom-call(bf16[4,2,384,1024]{3,2,1,0:T(8,128)(2,1)} %get-tuple-element.17.far, f32[2,384,1024]{2,1,0:T(8,128)} %get-tuple-element.18.own), custom_call_target="tpu_custom_call" | custom-call | bytes 150000000 | tf_op jit(solution)/shard_map/return_grads/pallas_call | solution.py:182
  168.6 0.0 copy-done.3
  168.6 0.0 copy-done.4
  168.6 0.0 copy-start.2
  168.6 1.9 convolution_convert_fusion.1
  170.5 0.0 copy-start.1
  170.5 9.9 %reduce-scatter.2.cloned.1.call-done = bf16[64,1024]{1,0:T(8,128)(2,1)} async-done(((bf16[1024,1024]{1,0:T(8,128)(2,1)}), bf16[64,1024]{1,0:T(8,128)(2,1)}) %reduce-scatter.2.cloned.1.call-update) | async-done | bytes 131088 | tf_op jit(solution)/shard_map/reduce_scatter | solution.py:344
  180.4 1.6 convert_multiply_fusion
  182.0 0.0 copy-done.2
  182.0 0.9 copy.15
  182.9 0.0 copy-done.1
  182.9 0.9 copy.16
Async XLA Ops:
  7.2 61.5 %copy-start = (bf16[384,1024]{1,0:T(8,128)(2,1)S(1)}, bf16[384,1024]{1,0:T(8,128)(2,1)}, u32[]{:S(2)}) copy-start(bf16[384,1024]{1,0:T(8,128)(2,1)} %param.12) | copy-start | bytes 2359300
  7.2 61.5 %all-gather.2.cloned.1.call-start = ((), (), s32[]{:S(2)}) async-start(), calls=%async_computation.1 | async-start | bytes 2228224 | tf_op jit(solution)/shard_map/all_gather | solution.py:326
  7.9 172.5 %reduce-scatter.2.cloned.1.call-start = ((), (), s32[]{:S(2)}) async-start(), calls=%async_computation.2 | async-start | bytes 2228224 | tf_op jit(solution)/shard_map/reduce_scatter | solution.py:344
  112.9 55.7 %copy-start.3 = (bf16[1024,1024]{1,0:T(8,128)(2,1)S(1)}, bf16[1024,1024]{1,0:T(8,128)(2,1)}, u32[]{:S(2)}) copy-start(bf16[1024,1024]{1,0:T(8,128)(2,1)} %all-gather.2.cloned.1.call-done) | copy-start | bytes 6291460
  112.9 55.7 %copy-start.4 = (bf16[384,1024]{1,0:T(8,128)(2,1)S(1)}, bf16[384,1024]{1,0:T(8,128)(2,1)}, u32[]{:S(2)}) copy-start(bf16[384,1024]{1,0:T(8,128)(2,1)} %get-tuple-element.15) | copy-start | bytes 2359300
  168.6 13.4 %copy-start.2 = (bf16[384,1024]{1,0:T(8,128)(2,1)S(1)}, bf16[384,1024]{1,0:T(8,128)(2,1)}, u32[]{:S(2)}) copy-start(bf16[384,1024]{1,0:T(8,128)(2,1)} %get-tuple-element.28) | copy-start | bytes 2359300
  170.5 12.4 %copy-start.1 = (bf16[384,1024]{1,0:T(8,128)(2,1)S(1)}, bf16[384,1024]{1,0:T(8,128)(2,1)}, u32[]{:S(2)}) copy-start(bf16[384,1024]{1,0:T(8,128)(2,1)} %get-tuple-element.29) | copy-start | bytes 2359300
Sparse Core Ops, SparseCore 0:
  10.2 50.1 all-gather.1
  113.0 67.3 reduce-scatter.1
where the time goes:
time: 194 us; the launch traced here: 191 us
  Pallas kernels  149 us (77%)
  between operations  14.1 us (7%)
  waiting for transfers between devices  10.6 us (5%)
  matrix products  9.07 us (5%)
  local copies, waits for them, and re-layouts  5.26 us (3%)
  other arithmetic  2.89 us (1%)
    pallas_call x1, Pallas kernels, gather_window(): pl.pallas_call(functools.partial(gather_kernel, n, chunks), out_shape=[sh...  57.2 us
    pallas_call x1, Pallas kernels, return_grads(): pl.pallas_call(functools.partial(return_kernel, n, chunks), out_shape=[sh...  55.6 us
    pallas_call x1, Pallas kernels, attention(): pl.pallas_call(functools.partial(attention_kernel, blocks, listed, block,...  35.7 us
    reduce_scatter x1, waiting for transfers between devices, shards(): lax.psum_scatter(lax.dot_general(attended, grad_output, (((0,), (0,)), ((...  9.93 us
  transfers between devices with their start and end apart: 2, of which 1 were waited for; matrix products, arithmetic and copies ran while one was open for 3% of the time, Pallas kernels for 59%

commit v1 on v0

v1 whole, which is shorter than its diff:
```python
import functools
import math

import jax
import jax.numpy as jnp
from jax import lax
from jax.experimental import pallas as pl
from jax.experimental.pallas import tpu as pltpu
from jax.sharding import PartitionSpec as P

HEADS = 16
REACH_DEV = 2
LANES = 128
AHEAD_KV = 3
AHEAD_W = 3


def layer_kernel(
    n, blocks, listed, block, head_dim, tokens,
    contacts, count, ids, q_hbm, k_hbm, v_hbm, w_hbm, g_hbm,
    mixed_hbm, dq_hbm, dk_hbm, dv_hbm, gw_hbm,
    q_v, k_v, v_v, g_v, wbuf, land, idt, bias, kwin, vwin, kg, vg, dks, dvs,
    own, far, got_f, got_c, got_z, got_y, put_z, put_y, outg, dqb, att_v, mix_v,
    gwp, core_got, gsum, rsbuf, ysend, ybuf, gfin, gwout, inv,
    local_sem, y_s, y_r, c_s, c_r, z_s, z_r, o_s, o_r,
    wy_s, w_s, w_r, wc_s, wc_r, ret_s, ret_r, gc_s, gc_r, gz_s, gz_r, gy_s, gy_r,
    out_sem, fin_sem,
):
    f32, bf16 = jnp.float32, jnp.bfloat16
    rows = blocks * block
    width = q_hbm.shape[1]
    pairs = width // LANES
    wrows = w_hbm.shape[0]
    nz = n // 4
    chips = LANES // (2 * wrows)
    reach = REACH_DEV * blocks
    windows = (2 * REACH_DEV + 1) * blocks
    scale = 1.0 / math.sqrt(head_dim)

    me = lax.axis_index("ctx")
    core, y, z = lax.rem(me, 2), lax.rem(me // 2, 2), me // 4
    ypeer, cpeer = me + 2 - 4 * y, me + 1 - 2 * core
    ahead, behind = me + 4 - 8 * y, me - 4 + 8 * y
    has_ahead = (ahead >= 0) & (ahead < n)
    has_behind = (behind >= 0) & (behind < n)

    def column(k):
        other = lax.rem(z + k, nz)
        return other, other * 4 + y * 2 + core

    def remote(src, dst, send, recv, device):
        return pltpu.make_async_remote_copy(
            src_ref=src, dst_ref=dst, send_sem=send, recv_sem=recv,
            device_id={"ctx": device}, device_id_type=pl.DeviceIdType.MESH,
        )

    def over(start, stop, body):
        lax.fori_loop(start, stop, lambda i, c: (body(i), c)[1], 0)

    def lanes(p):
        return pl.ds(pl.multiple_of(p * LANES, LANES), LANES)

    def shard(d):
        return pl.ds(pl.multiple_of(d * wrows, wrows), wrows)

    def kv_y(a, p):
        return remote(
            (k_hbm, v_hbm)[a].at[:, lanes(p)], land.at[p, 3 * y, a], y_s.at[a, p], y_r.at[a, p], ypeer
        )

    def kv_c(a, p):
        return remote(
            (k_hbm, v_hbm)[a].at[:, lanes(p)], land.at[p, 1 + core, a], c_s.at[a, p], c_r.at[a, p], cpeer
        )

    def kv_z(p):
        return remote(land.at[p, 3 - 3 * y], land.at[p, 3 * y], z_s.at[p], z_r.at[p], ahead)

    def kv_on(p):
        return remote(land.at[p, 3 - 3 * core], land.at[p, 2 - core], o_s.at[p], o_r.at[p], cpeer)

    on_sent = (y == core) | has_behind
    on_got = (y != core) | has_behind

    def kv_start(p):
        for a in range(2):
            kv_y(a, p).start()
        for a in range(2):
            kv_c(a, p).start()

    def kv_first(p):
        for a in range(2):
            kv_y(a, p).wait_recv()
        pl.when(has_ahead)(lambda: kv_z(p).start())
        pl.when(y == core)(lambda: kv_on(p).start())

    def kv_second(p):
        @pl.when(has_behind)
        def _():
            kv_z(p).wait_recv()
            pl.when(y != core)(lambda: kv_on(p).start())

    def kv_wait(p):
        for a in range(2):
            kv_c(a, p).wait_recv()
        pl.when(on_got)(lambda: kv_on(p).wait_recv())

    mychip, ychip = me // 2, me // 2 + 1 - 2 * y

    def w_y():
        return remote(w_hbm, wbuf.at[shard(me)], wy_s, w_r.at[mychip], ypeer)

    def w_in(chip):
        d = shard(2 * chip + core)
        return remote(wbuf.at[d], wbuf.at[d], wy_s, w_r.at[chip], ypeer)

    def w_z(mine, k):
        _, device = column(k)
        if mine:
            return remote(w_hbm, wbuf.at[shard(me)], w_s.at[0, k], w_r.at[mychip], device)
        d = shard(2 * ychip + core)
        return remote(wbuf.at[d], wbuf.at[d], w_s.at[1, k], w_r.at[ychip], device)

    def w_c(chip):
        d = shard(2 * chip + core)
        return remote(wbuf.at[d], wbuf.at[d], wc_s.at[chip], wc_r.at[chip], cpeer)

    def w_send(p):
        for i in range(chips):
            chip = p * chips + i

            @pl.when(chip == mychip)
            def _():
                over(1, nz, lambda k: w_z(True, k).start())

            @pl.when(chip == ychip)
            def _():
                w_in(ychip).wait_recv()
                over(1, nz, lambda k: w_z(False, k).start())

    def w_forward(p):
        for i in range(chips):
            chip = p * chips + i
            pl.when((chip != mychip) & (chip != ychip))(lambda chip=chip: w_in(chip).wait_recv())
            w_c(chip).start()

    def w_wait(p):
        for i in range(chips):
            w_c(p * chips + i).wait_recv()

    def back(p):
        return remote(far.at[p, 1 + core], got_f.at[p], ret_s.at[0, p], ret_r.at[0, p], cpeer)

    def across(p):
        return remote(far.at[p, 2 - core], got_c.at[p], ret_s.at[1, p], ret_r.at[1, p], cpeer)

    def ret_z(p):
        return remote(put_z.at[p], got_z.at[p], ret_s.at[2, p], ret_r.at[2, p], behind)

    def ret_y(p):
        return remote(put_y.at[p], got_y.at[p], ret_s.at[3, p], ret_r.at[3, p], ypeer)

    sent_back = (y != core) | has_behind
    got_back = (y == core) | has_behind

    def ret_one(p):
        pl.when(sent_back)(lambda: back(p).start())
        across(p).start()

    def ret_two(p):
        pl.when(got_back)(lambda: back(p).wait_recv())
        value = far[p, 3 * y].astype(f32)
        put_z[p] = (value + jnp.where(y != core, got_f[p].astype(f32), 0.0)).astype(bf16)
        pl.when(has_behind)(lambda: ret_z(p).start())

    def ret_three(p):
        pl.when(has_ahead)(lambda: ret_z(p).wait_recv())
        value = far[p, 3 - 3 * y].astype(f32)
        value = value + jnp.where(has_ahead, got_z[p].astype(f32), 0.0)
        value = value + jnp.where(y == core, got_f[p].astype(f32), 0.0)
        put_y[p] = value.astype(bf16)
        ret_y(p).start()

    def out_copy(a, p):
        src = dqb.at[p] if a == 2 else outg.at[p, a]
        return pltpu.make_async_copy(src, (dk_hbm, dv_hbm, dq_hbm)[a].at[:, lanes(p)], out_sem.at[a, p])

    def ret_four(p):
        across(p).wait_recv()
        ret_y(p).wait_recv()
        outg[p] = (own[p] + got_c[p].astype(f32) + got_y[p].astype(f32)).astype(bf16)
        for a in range(2):
            out_copy(a, p).start()

    def gw_c(chip):
        return remote(
            gwp.at[shard(2 * chip + 1 - core)], core_got.at[chip], gc_s.at[chip], gc_r.at[chip], cpeer
        )

    def gw_z(chip):
        zc, yc = chip // 2, lax.rem(chip, 2)
        return remote(gsum.at[chip], rsbuf.at[yc, z], gz_s.at[chip], gz_r.at[yc, z], zc * 4 + y * 2 + core)

    def gw_in(yc, other):
        return remote(gsum.at[0], rsbuf.at[yc, other], gz_s.at[0], gz_r.at[yc, other], ypeer)

    def gw_y():
        return remote(ysend, ybuf, gy_s, gy_r, ypeer)

    def gw_one(p):
        for i in range(chips):
            gw_c(p * chips + i).start()

    def gw_two(p):
        for i in range(chips):
            chip = p * chips + i
            zc, yc = chip // 2, lax.rem(chip, 2)
            gw_c(chip).wait_recv()
            value = gwp[shard(2 * chip + core), :].astype(f32) + core_got[chip].astype(f32)
            gsum[chip] = value.astype(bf16)
            pl.when(zc != z)(lambda chip=chip: gw_z(chip).start())

            @pl.when(zc == z)
            def _(value=value, yc=yc):
                rsbuf[yc, z] = value.astype(bf16)

    def gw_three(p):
        for i in range(chips):
            chip = p * chips + i
            yc = lax.rem(chip, 2)

            @pl.when(chip // 2 == z)
            def _(yc=yc):
                over(1, nz, lambda k: gw_in(yc, column(k)[0]).wait_recv())
                value = rsbuf[yc, 0].astype(f32)
                for other in range(1, nz):
                    value = value + rsbuf[yc, other].astype(f32)

                @pl.when(yc == y)
                def _():
                    gfin[...] = value

                @pl.when(yc != y)
                def _():
                    ysend[...] = value.astype(bf16)
                    gw_y().start()

    barrier = pltpu.get_barrier_semaphore()

    def hello(device):
        pl.semaphore_signal(barrier, inc=1, device_id={"ctx": device}, device_id_type=pl.DeviceIdType.MESH)

    hello(ypeer)
    hello(cpeer)
    over(1, nz, lambda k: hello(column(k)[1]))
    pl.semaphore_wait(barrier, nz + 1)

    w_y().start()
    kv_start(0)
    loads = [
        pltpu.make_async_copy(w_hbm, wbuf.at[shard(me)], local_sem.at[0]),
        pltpu.make_async_copy(g_hbm, g_v, local_sem.at[1]),
        pltpu.make_async_copy(q_hbm, q_v, local_sem.at[2]),
        pltpu.make_async_copy(k_hbm, k_v, local_sem.at[3]),
        pltpu.make_async_copy(v_hbm, v_v, local_sem.at[4]),
    ]
    for copy in loads:
        copy.start()
    for p in range(1, AHEAD_KV):
        kv_start(p)
    for p in range(AHEAD_W):
        w_send(p)

    first = me * blocks - reach
    total_blocks = ids.shape[0]
    for w in range(windows):
        at = jnp.clip(first + w, 0, total_blocks - 1)
        row = ids[pl.ds(at, 1), :].astype(f32)
        idt[w] = jnp.broadcast_to(row, (block, block)).T
    local = [[jnp.clip(contacts[b, j] - first, 0, windows - 1) for j in range(listed)] for b in range(blocks)]
    for b in range(blocks):
        mine = ids[pl.ds(me * blocks + b, 1), :].astype(f32)
        for j in range(listed):
            same = idt[local[b][j]] == mine
            alive = jnp.full((block, LANES), count[b], jnp.int32) > j
            bias[pl.ds((b * listed + j) * block, block), :] = jnp.where(same & alive, 0.0, -jnp.inf)
        for w in range(2 * reach + 1):
            slot = jnp.int32(blocks * listed)
            for j in range(listed):
                slot = jnp.where(local[b][j] == w + b, b * listed + j, slot)
            inv[b, w] = slot
    for ref in (dks, dvs):
        ref[blocks * listed] = jnp.zeros((block, LANES), f32)
    for copy in loads:
        copy.wait()

    lane = lax.broadcasted_iota(jnp.int32, (block, LANES), 1) < head_dim
    sub = lax.broadcasted_iota(jnp.int32, (LANES, block), 0) < head_dim
    last_dim = (((1,), (1,)), ((), ()))
    first_dim = (((0,), (0,)), ((), ()))

    def two(x):
        zero = jnp.zeros_like(x)
        return jnp.concatenate([jnp.where(lane, x, zero), jnp.where(lane, zero, x)], axis=0).astype(bf16)

    def attend(p):
        cols = lanes(p)
        grad_all = lax.dot_general(
            g_v[...], wbuf[cols, :], last_dim, preferred_element_type=f32
        ).astype(bf16)
        for i, piece in enumerate((0, 1, None, 2, 3)):
            span = pl.ds(i * blocks, blocks)
            kwin[span] = (k_v[:, cols] if piece is None else land[p, piece, 0]).reshape(blocks, block, LANES)
            vwin[span] = (v_v[:, cols] if piece is None else land[p, piece, 1]).reshape(blocks, block, LANES)
        for b in range(blocks):
            here = pl.ds(b * block, block)
            for j in range(listed):
                at = jnp.clip(contacts[b, j] - first, 0, windows - 1)
                kg[pl.ds(j * block, block), :] = kwin[at]
                vg[pl.ds(j * block, block), :] = vwin[at]
            grad = grad_all[b * block : (b + 1) * block].astype(f32)
            q2 = two(q_v[here, cols].astype(f32) * scale)
            d2 = two(grad)
            s = lax.dot_general(kg[...], q2, last_dim, preferred_element_type=f32)
            mask = bias[pl.ds(b * listed * block, listed * block), :]
            s = s + jnp.concatenate([mask, mask], axis=1)
            top = jnp.max(s, axis=0, keepdims=True)
            e = jnp.exp(s - top)
            probs = e * (1.0 / jnp.sum(e, axis=0, keepdims=True))
            low = probs.astype(bf16)
            ot = lax.dot_general(vg[...], low, first_dim, preferred_element_type=f32)
            att = jnp.where(sub, ot[:, :block], ot[:, block:]).astype(bf16).astype(f32)
            att_v[here, cols] = att.T.astype(bf16)
            prod = grad.T * att
            row_dot = jnp.concatenate(
                [jnp.sum(prod[:head_dim], axis=0, keepdims=True), jnp.sum(prod[head_dim:], axis=0, keepdims=True)],
                axis=1,
            )
            dp = lax.dot_general(vg[...], d2, last_dim, preferred_element_type=f32)
            ds = (probs * (dp - row_dot)).astype(bf16)
            dqt = lax.dot_general(kg[...], ds, first_dim, preferred_element_type=f32)
            dq = jnp.where(sub, dqt[:, :block], dqt[:, block:]) * scale
            dqb[p, here, :] = dq.T.astype(bf16)
            part = pl.ds(b * listed, listed)
            dks[part] = jnp.dot(ds, q2, preferred_element_type=f32).reshape(listed, block, LANES)
            dvs[part] = jnp.dot(low, d2, preferred_element_type=f32).reshape(listed, block, LANES)
        out_copy(2, p).start()
        for a, slots in enumerate((dks, dvs)):
            for w in range(windows):
                value = None
                for b in range(blocks):
                    if 0 <= w - b <= 2 * reach:
                        term = slots[inv[b, w - b]]
                        value = term if value is None else value + term
                piece, part = w // blocks, pl.ds((w % blocks) * block, block)
                if piece == REACH_DEV:
                    own[p, a, part, :] = value
                else:
                    far[p, piece - (piece > REACH_DEV), a, part, :] = value.astype(bf16)
        ret_one(p)
        gwp[cols, :] = lax.dot_general(
            att_v[:, cols], g_v[...], first_dim, preferred_element_type=f32
        ).astype(bf16)
        gw_one(p)

    kv_first(0)
    kv_first(1)
    kv_second(0)
    w_forward(0)

    def step(p):
        pl.when(p + AHEAD_KV < pairs)(lambda: kv_start(p + AHEAD_KV))
        pl.when(p + 2 < pairs)(lambda: kv_first(p + 2))

        @pl.when(p + 1 < pairs)
        def _():
            kv_second(p + 1)
            w_forward(p + 1)

        pl.when(p + AHEAD_W < pairs)(lambda: w_send(p + AHEAD_W))

        @pl.when(p < pairs)
        def _():
            kv_wait(p)
            w_wait(p)
            attend(p)

        @pl.when((p >= 1) & (p <= pairs))
        def _():
            ret_two(p - 1)
            gw_two(p - 1)

        pl.when((p >= 2) & (p <= pairs + 1))(lambda: ret_three(p - 2))

        @pl.when(p == pairs)
        def _():
            mix_v[...] = jnp.dot(att_v[...], wbuf[...], preferred_element_type=f32).astype(bf16)
            pltpu.make_async_copy(mix_v, mixed_hbm, fin_sem.at[0]).start()

        @pl.when(p >= 3)
        def _():
            ret_four(p - 3)
            gw_three(p - 3)

    over(0, pairs + 3, step)

    gw_y().wait_recv()
    gwout[...] = (gfin[...] + ybuf[...].astype(f32)) * jnp.float32(1.0 / math.sqrt(tokens))
    pltpu.make_async_copy(gwout, gw_hbm, fin_sem.at[1]).start()

    w_y().wait_send()
    for mine in (True, False):
        over(1, nz, lambda k: w_z(mine, k).wait_send())

    def sent(p):
        for a in range(2):
            kv_y(a, p).wait_send()
            kv_c(a, p).wait_send()
        pl.when(has_ahead)(lambda: kv_z(p).wait_send())
        pl.when(on_sent)(lambda: kv_on(p).wait_send())
        pl.when(sent_back)(lambda: back(p).wait_send())
        across(p).wait_send()
        pl.when(has_behind)(lambda: ret_z(p).wait_send())
        ret_y(p).wait_send()
        for a in range(3):
            out_copy(a, p).wait()
        for i in range(chips):
            chip = p * chips + i
            w_c(chip).wait_send()
            gw_c(chip).wait_send()
            pl.when(chip // 2 != z)(lambda chip=chip: gw_z(chip).wait_send())

    over(0, pairs, sent)
    gw_y().wait_send()
    pltpu.make_async_copy(mix_v, mixed_hbm, fin_sem.at[0]).wait()
    pltpu.make_async_copy(gwout, gw_hbm, fin_sem.at[1]).wait()


def layer(contacts, count, ids, queries, keys, values, weight, grad_output):
    n = lax.axis_size("ctx")
    rows, width = queries.shape
    blocks, listed = contacts.shape
    block = rows // blocks
    wrows = weight.shape[0]
    pairs, nz = width // LANES, n // 4
    window = (2 * REACH_DEV + 1) * blocks
    f32, bf16 = jnp.float32, jnp.bfloat16
    vmem, dma = pltpu.VMEM, pltpu.SemaphoreType.DMA
    smem = pl.BlockSpec(memory_space=pltpu.SMEM)
    hbm = pl.BlockSpec(memory_space=pl.ANY)
    slots = blocks * listed + 1
    flat, both = (rows, width), (pairs, 2, rows, LANES)
    return pl.pallas_call(
        functools.partial(layer_kernel, n, blocks, listed, block, width // HEADS, rows * n),
        in_specs=[smem, smem, pl.BlockSpec(memory_space=pltpu.VMEM)] + [hbm] * 5,
        out_specs=[hbm] * 5,
        out_shape=[jax.ShapeDtypeStruct(flat, bf16)] * 4 + [jax.ShapeDtypeStruct((wrows, width), f32)],
        scratch_shapes=[vmem(flat, bf16)] * 4
        + [
            vmem((width, width), bf16),
            vmem((pairs, 2 * REACH_DEV, 2, rows, LANES), bf16),
            vmem((window, block, block), f32),
            vmem((blocks * listed * block, LANES), f32),
            vmem((window, block, LANES), bf16),
            vmem((window, block, LANES), bf16),
            vmem((listed * block, LANES), bf16),
            vmem((listed * block, LANES), bf16),
            vmem((slots, block, LANES), f32),
            vmem((slots, block, LANES), f32),
            vmem(both, f32),
            vmem((pairs, 2 * REACH_DEV, 2, rows, LANES), bf16),
        ]
        + [vmem(both, bf16)] * 7
        + [
            vmem((pairs, rows, LANES), bf16),
            vmem(flat, bf16),
            vmem(flat, bf16),
            vmem((width, width), bf16),
            vmem((n // 2, wrows, width), bf16),
            vmem((n // 2, wrows, width), bf16),
            vmem((2, nz, wrows, width), bf16),
            vmem((wrows, width), bf16),
            vmem((wrows, width), bf16),
            vmem((wrows, width), f32),
            vmem((wrows, width), f32),
            pltpu.SMEM((blocks, 2 * REACH_DEV * blocks + 1), jnp.int32),
            dma((5,)),
        ]
        + [dma((2, pairs))] * 4
        + [dma((pairs,))] * 4
        + [dma, dma((2, nz))]
        + [dma((n // 2,))] * 3
        + [dma((4, pairs))] * 2
        + [dma((n // 2,))] * 3
        + [dma((2, nz)), dma, dma, dma((3, pairs)), dma((2,))],
        compiler_params=pltpu.CompilerParams(
            collective_id=0, has_side_effects=True, vmem_limit_bytes=60 * 1024 * 1024
        ),
        name="contact_layer",
    )(contacts, count, ids, queries, keys, values, weight, grad_output)


def shards(queries, keys, values, out_weight, grad_output, complex_id, contacts, contact_count):
    block = queries.shape[0] // contacts.shape[0]
    return layer(
        contacts, contact_count, complex_id.reshape(-1, block), queries, keys, values, out_weight, grad_output
    )


def solution(mesh):
    split = P(("groups", "ctx"), None)
    return jax.shard_map(
        shards,
        mesh=mesh,
        in_specs=(split, split, split, P("ctx", None), split, P("groups"), split, P(("groups", "ctx"))),
        out_specs=(split,) * 5,
        check_vma=False,
    )
```

time: 194 us -> 149 us (0.77)
  the two profiles are of different devices: /device:TPU:22 before, /device:TPU:28 now
where the time goes in v1:
time: 149 us
  Pallas kernels  142 us (95%)
  local copies, waits for them, and re-layouts  6.77 us (5%)
    pallas_call x1, Pallas kernels, layer(): pl.pallas_call(functools.partial(layer_kernel, n, blocks, listed, block,...  142 us
    unnamed x13, local copies, waits for them, and re-layouts  6.77 us

profile of v1, /device:TPU:28, one launch (start us, length us, event | category | flops | bytes accessed | tf_op | source)
XLA Modules:
  0.0 149.1 jit_solution(16062266129788383002)
XLA Ops:
  0.6 141.7 %contact_layer.1 = (bf16[384,1024]{1,0:T(8,128)(2,1)}, bf16[384,1024]{1,0:T(8,128)(2,1)}, bf16[384,1024]{1,0:T(8,128)(2,1)}, bf16[384,1024]{1,0:T(8,128)(2,1)}, f32[64,1024]{1,0:T(8,128)}) custom-call(s32[3,6]{1,0:T(4,128)} %contacts.1, s32[3]{0:T(128)} %count.1, s32[48,128]{1,0:T(8,128)} %bitcast.1, bf16[384,1024]{1,0:T(8,128)(2,1)} %q_hbm.1, ...), custom_call_target="tpu_custom_call" | custom-call | tf_op jit(solution)/shard_map/contact_layer/pallas_call | solution.py:453
  142.4 0.0 copy-start.2
  142.4 2.1 %copy.18 = bf16[384,1024]{1,0:T(8,128)(2,1)} copy(bf16[384,1024]{1,0:T(8,128)(2,1)} %get-tuple-element.10) | data formatting | bytes 1572864
  144.5 0.0 copy-done.2
  144.5 0.0 copy-start.1
  144.5 0.9 copy.19
  145.4 0.5 copy-done.1
  145.9 0.0 copy-start
  145.9 0.9 copy.20
  146.8 0.5 copy-done
  147.4 0.0 copy-start.3
  147.4 0.9 copy.21
  148.2 0.2 copy-done.3
  148.4 0.7 copy.22
Async XLA Ops:
  142.4 2.1 %copy-start.2 = (bf16[384,1024]{1,0:T(8,128)(2,1)S(1)}, bf16[384,1024]{1,0:T(8,128)(2,1)}, u32[]{:S(2)}) copy-start(bf16[384,1024]{1,0:T(8,128)(2,1)} %get-tuple-element.11) | copy-start | bytes 2359300
  144.5 1.4 copy-start.1
  145.9 1.4 copy-start
  147.4 1.1 copy-start.3

commit v2 on v1

--- a/solution.py
+++ b/solution.py
@@ -12,7 +12,7 @@
 REACH_DEV = 2
 LANES = 128
 AHEAD_KV = 3
-AHEAD_W = 3
+LEAD = 4
 
 
 def layer_kernel(
@@ -21,7 +21,7 @@
     mixed_hbm, dq_hbm, dk_hbm, dv_hbm, gw_hbm,
     q_v, k_v, v_v, g_v, wbuf, land, idt, bias, kwin, vwin, kg, vg, dks, dvs,
     own, far, got_f, got_c, got_z, got_y, put_z, put_y, outg, dqb, att_v, mix_v,
-    gwp, core_got, gsum, rsbuf, ysend, ybuf, gfin, gwout, inv,
+    gwp, core_got, gsum, gin, ysend, ybuf, gfin, gwout, inv,
     local_sem, y_s, y_r, c_s, c_r, z_s, z_r, o_s, o_r,
     wy_s, w_s, w_r, wc_s, wc_r, ret_s, ret_r, gc_s, gc_r, gz_s, gz_r, gy_s, gy_r,
     out_sem, fin_sem,
@@ -44,10 +44,6 @@
     has_ahead = (ahead >= 0) & (ahead < n)
     has_behind = (behind >= 0) & (behind < n)
 
-    def column(k):
-        other = lax.rem(z + k, nz)
-        return other, other * 4 + y * 2 + core
-
     def remote(src, dst, send, recv, device):
         return pltpu.make_async_remote_copy(
             src_ref=src, dst_ref=dst, send_sem=send, recv_sem=recv,
@@ -57,8 +53,11 @@
     def over(start, stop, body):
         lax.fori_loop(start, stop, lambda i, c: (body(i), c)[1], 0)
 
+    def turn(p):
+        return p + 2 - 4 * lax.rem(p // 2, 2)
+
     def lanes(p):
-        return pl.ds(pl.multiple_of(p * LANES, LANES), LANES)
+        return pl.ds(pl.multiple_of(turn(p) * LANES, LANES), LANES)
 
     def shard(d):
         return pl.ds(pl.multiple_of(d * wrows, wrows), wrows)
@@ -105,7 +104,7 @@
             kv_c(a, p).wait_recv()
         pl.when(on_got)(lambda: kv_on(p).wait_recv())
 
-    mychip, ychip = me // 2, me // 2 + 1 - 2 * y
+    mychip = me // 2
 
     def w_y():
         return remote(w_hbm, wbuf.at[shard(me)], wy_s, w_r.at[mychip], ypeer)
@@ -114,39 +113,34 @@
         d = shard(2 * chip + core)
         return remote(wbuf.at[d], wbuf.at[d], wy_s, w_r.at[chip], ypeer)
 
-    def w_z(mine, k):
-        _, device = column(k)
-        if mine:
-            return remote(w_hbm, wbuf.at[shard(me)], w_s.at[0, k], w_r.at[mychip], device)
-        d = shard(2 * ychip + core)
-        return remote(wbuf.at[d], wbuf.at[d], w_s.at[1, k], w_r.at[ychip], device)
+    def w_z(chip, up):
+        d = shard(2 * chip + core)
+        return remote(wbuf.at[d], wbuf.at[d], w_s.at[up, chip], w_r.at[chip], me - 4 + 8 * up)
 
     def w_c(chip):
         d = shard(2 * chip + core)
         return remote(wbuf.at[d], wbuf.at[d], wc_s.at[chip], wc_r.at[chip], cpeer)
 
-    def w_send(p):
+    def w_goes(chip):
+        zc = chip // 2
+        return (z >= zc) & (z + 1 < nz), (z <= zc) & (z > 0)
+
+    def w_hop(p, lead):
         for i in range(chips):
-            chip = p * chips + i
-
-            @pl.when(chip == mychip)
-            def _():
-                over(1, nz, lambda k: w_z(True, k).start())
-
-            @pl.when(chip == ychip)
-            def _():
-                w_in(ychip).wait_recv()
-                over(1, nz, lambda k: w_z(False, k).start())
-
-    def w_forward(p):
-        for i in range(chips):
-            chip = p * chips + i
-            pl.when((chip != mychip) & (chip != ychip))(lambda chip=chip: w_in(chip).wait_recv())
-            w_c(chip).start()
+            chip = turn(p) * chips + i
+            far_off = jnp.abs(z - chip // 2)
+
+            @pl.when(jnp.maximum(1, LEAD - far_off) == lead)
+            def _(chip=chip):
+                up, down = w_goes(chip)
+                pl.when(chip != mychip)(lambda: w_in(chip).wait_recv())
+                pl.when(up)(lambda: w_z(chip, 1).start())
+                pl.when(down)(lambda: w_z(chip, 0).start())
+                w_c(chip).start()
 
     def w_wait(p):
         for i in range(chips):
-            w_c(p * chips + i).wait_recv()
+            w_c(turn(p) * chips + i).wait_recv()
 
     def back(p):
         return remote(far.at[p, 1 + core], got_f.at[p], ret_s.at[0, p], ret_r.at[0, p], cpeer)
@@ -198,43 +192,52 @@
         )
 
     def gw_z(chip):
-        zc, yc = chip // 2, lax.rem(chip, 2)
-        return remote(gsum.at[chip], rsbuf.at[yc, z], gz_s.at[chip], gz_r.at[yc, z], zc * 4 + y * 2 + core)
-
-    def gw_in(yc, other):
-        return remote(gsum.at[0], rsbuf.at[yc, other], gz_s.at[0], gz_r.at[yc, other], ypeer)
+        side = (z > chip // 2).astype(jnp.int32)
+        return remote(
+            gsum.at[chip], gin.at[side, chip], gz_s.at[chip], gz_r.at[side, chip], me + 4 - 8 * side
+        )
+
+    def gw_in(chip, side):
+        return remote(gsum.at[chip], gin.at[side, chip], gz_s.at[chip], gz_r.at[side, chip], ypeer)
 
     def gw_y():
         return remote(ysend, ybuf, gy_s, gy_r, ypeer)
 
     def gw_one(p):
         for i in range(chips):
-            gw_c(p * chips + i).start()
+            gw_c(turn(p) * chips + i).start()
 
     def gw_two(p):
         for i in range(chips):
-            chip = p * chips + i
-            zc, yc = chip // 2, lax.rem(chip, 2)
+            chip = turn(p) * chips + i
+            zc = chip // 2
             gw_c(chip).wait_recv()
             value = gwp[shard(2 * chip + core), :].astype(f32) + core_got[chip].astype(f32)
             gsum[chip] = value.astype(bf16)
-            pl.when(zc != z)(lambda chip=chip: gw_z(chip).start())
-
-            @pl.when(zc == z)
-            def _(value=value, yc=yc):
-                rsbuf[yc, z] = value.astype(bf16)
-
-    def gw_three(p):
+            ends = ((z == 0) & (zc > 0)) | ((z == nz - 1) & (zc < nz - 1))
+            pl.when(ends)(lambda chip=chip: gw_z(chip).start())
+
+    def gw_hop(p, lag):
         for i in range(chips):
-            chip = p * chips + i
-            yc = lax.rem(chip, 2)
-
-            @pl.when(chip // 2 == z)
-            def _(yc=yc):
-                over(1, nz, lambda k: gw_in(yc, column(k)[0]).wait_recv())
-                value = rsbuf[yc, 0].astype(f32)
-                for other in range(1, nz):
-                    value = value + rsbuf[yc, other].astype(f32)
+            chip = turn(p) * chips + i
+            zc = chip // 2
+            stage = jnp.where(z < zc, z, nz - 1 - z)
+
+            @pl.when((z != zc) & (stage > 0) & (jnp.minimum(stage + 1, LEAD - 1) == lag))
+            def _(chip=chip, zc=zc):
+                side = (z > zc).astype(jnp.int32)
+                gw_in(chip, side).wait_recv()
+                gsum[chip] = (gsum[chip].astype(f32) + gin[side, chip].astype(f32)).astype(bf16)
+                gw_z(chip).start()
+
+            @pl.when((z == zc) & (jnp.minimum(jnp.maximum(zc, nz - 1 - zc) + 1, LEAD) == lag))
+            def _(chip=chip):
+                yc = lax.rem(chip, 2)
+                pl.when(z > 0)(lambda: gw_in(chip, 0).wait_recv())
+                pl.when(z < nz - 1)(lambda: gw_in(chip, 1).wait_recv())
+                value = gsum[chip].astype(f32)
+                value = value + jnp.where(z > 0, gin[0, chip].astype(f32), 0.0)
+                value = value + jnp.where(z < nz - 1, gin[1, chip].astype(f32), 0.0)
 
                 @pl.when(yc == y)
                 def _():
@@ -252,8 +255,9 @@
 
     hello(ypeer)
     hello(cpeer)
-    over(1, nz, lambda k: hello(column(k)[1]))
-    pl.semaphore_wait(barrier, nz + 1)
+    pl.when(z > 0)(lambda: hello(me - 4))
+    pl.when(z < nz - 1)(lambda: hello(me + 4))
+    pl.semaphore_wait(barrier, 2 + (z > 0).astype(jnp.int32) + (z < nz - 1).astype(jnp.int32))
 
     w_y().start()
     kv_start(0)
@@ -268,31 +272,32 @@
         copy.start()
     for p in range(1, AHEAD_KV):
         kv_start(p)
-    for p in range(AHEAD_W):
-        w_send(p)
+    loads[0].wait()
 
     first = me * blocks - reach
-    total_blocks = ids.shape[0]
-    for w in range(windows):
-        at = jnp.clip(first + w, 0, total_blocks - 1)
-        row = ids[pl.ds(at, 1), :].astype(f32)
-        idt[w] = jnp.broadcast_to(row, (block, block)).T
-    local = [[jnp.clip(contacts[b, j] - first, 0, windows - 1) for j in range(listed)] for b in range(blocks)]
-    for b in range(blocks):
-        mine = ids[pl.ds(me * blocks + b, 1), :].astype(f32)
-        for j in range(listed):
-            same = idt[local[b][j]] == mine
-            alive = jnp.full((block, LANES), count[b], jnp.int32) > j
-            bias[pl.ds((b * listed + j) * block, block), :] = jnp.where(same & alive, 0.0, -jnp.inf)
-        for w in range(2 * reach + 1):
-            slot = jnp.int32(blocks * listed)
+
+    def setup():
+        total_blocks = ids.shape[0]
+        for w in range(windows):
+            at = jnp.clip(first + w, 0, total_blocks - 1)
+            row = ids[pl.ds(at, 1), :].astype(f32)
+            idt[w] = jnp.broadcast_to(row, (block, block)).T
+        local = [[jnp.clip(contacts[b, j] - first, 0, windows - 1) for j in range(listed)] for b in range(blocks)]
+        for b in range(blocks):
+            mine = ids[pl.ds(me * blocks + b, 1), :].astype(f32)
             for j in range(listed):
-                slot = jnp.where(local[b][j] == w + b, b * listed + j, slot)
-            inv[b, w] = slot
-    for ref in (dks, dvs):
-        ref[blocks * listed] = jnp.zeros((block, LANES), f32)
-    for copy in loads:
-        copy.wait()
+                same = idt[local[b][j]] == mine
+                alive = jnp.full((block, LANES), count[b], jnp.int32) > j
+                bias[pl.ds((b * listed + j) * block, block), :] = jnp.where(same & alive, 0.0, -jnp.inf)
+            for w in range(2 * reach + 1):
+                slot = jnp.int32(blocks * listed)
+                for j in range(listed):
+                    slot = jnp.where(local[b][j] == w + b, b * listed + j, slot)
+                inv[b, w] = slot
+        for ref in (dks, dvs):
+            ref[blocks * listed] = jnp.zeros((block, LANES), f32)
+        for copy in loads[1:]:
+            copy.wait()
 
     lane = lax.broadcasted_iota(jnp.int32, (block, LANES), 1) < head_dim
     sub = lax.broadcasted_iota(jnp.int32, (LANES, block), 0) < head_dim
@@ -363,54 +368,43 @@
         ).astype(bf16)
         gw_one(p)
 
-    kv_first(0)
-    kv_first(1)
-    kv_second(0)
-    w_forward(0)
+    def among(q, body):
+        pl.when((q >= 0) & (q < pairs))(lambda: body(q))
 
     def step(p):
-        pl.when(p + AHEAD_KV < pairs)(lambda: kv_start(p + AHEAD_KV))
-        pl.when(p + 2 < pairs)(lambda: kv_first(p + 2))
-
-        @pl.when(p + 1 < pairs)
-        def _():
-            kv_second(p + 1)
-            w_forward(p + 1)
-
-        pl.when(p + AHEAD_W < pairs)(lambda: w_send(p + AHEAD_W))
-
-        @pl.when(p < pairs)
+        pl.when((p >= 0) & (p + AHEAD_KV < pairs))(lambda: kv_start(p + AHEAD_KV))
+        among(p + 2, kv_first)
+        among(p + 1, kv_second)
+        for lead in range(LEAD, 0, -1):
+            among(p + lead, lambda q, lead=lead: w_hop(q, lead))
+        pl.when(p == -2)(setup)
+
+        @pl.when((p >= 0) & (p < pairs))
         def _():
             kv_wait(p)
             w_wait(p)
             attend(p)
 
-        @pl.when((p >= 1) & (p <= pairs))
-        def _():
-            ret_two(p - 1)
-            gw_two(p - 1)
-
-        pl.when((p >= 2) & (p <= pairs + 1))(lambda: ret_three(p - 2))
+        among(p - 1, ret_two)
+        among(p - 1, gw_two)
+        among(p - 2, ret_three)
 
         @pl.when(p == pairs)
         def _():
             mix_v[...] = jnp.dot(att_v[...], wbuf[...], preferred_element_type=f32).astype(bf16)
             pltpu.make_async_copy(mix_v, mixed_hbm, fin_sem.at[0]).start()
 
-        @pl.when(p >= 3)
-        def _():
-            ret_four(p - 3)
-            gw_three(p - 3)
-
-    over(0, pairs + 3, step)
+        among(p - 3, ret_four)
+        for lag in range(2, LEAD + 1):
+            among(p - lag, lambda q, lag=lag: gw_hop(q, lag))
+
+    over(-LEAD, pairs + LEAD, step)
 
     gw_y().wait_recv()
     gwout[...] = (gfin[...] + ybuf[...].astype(f32)) * jnp.float32(1.0 / math.sqrt(tokens))
     pltpu.make_async_copy(gwout, gw_hbm, fin_sem.at[1]).start()
 
     w_y().wait_send()
-    for mine in (True, False):
-        over(1, nz, lambda k: w_z(mine, k).wait_send())
 
     def sent(p):
         for a in range(2):
@@ -426,6 +420,9 @@
             out_copy(a, p).wait()
         for i in range(chips):
             chip = p * chips + i
+            up, down = w_goes(chip)
+            pl.when(up)(lambda chip=chip: w_z(chip, 1).wait_send())
+            pl.when(down)(lambda chip=chip: w_z(chip, 0).wait_send())
             w_c(chip).wait_send()
             gw_c(chip).wait_send()
             pl.when(chip // 2 != z)(lambda chip=chip: gw_z(chip).wait_send())
@@ -442,7 +439,7 @@
     blocks, listed = contacts.shape
     block = rows // blocks
     wrows = weight.shape[0]
-    pairs, nz = width // LANES, n // 4
+    pairs = width // LANES
     window = (2 * REACH_DEV + 1) * blocks
     f32, bf16 = jnp.float32, jnp.bfloat16
     vmem, dma = pltpu.VMEM, pltpu.SemaphoreType.DMA
@@ -478,7 +475,7 @@
             vmem((width, width), bf16),
             vmem((n // 2, wrows, width), bf16),
             vmem((n // 2, wrows, width), bf16),
-            vmem((2, nz, wrows, width), bf16),
+            vmem((2, n // 2, wrows, width), bf16),
             vmem((wrows, width), bf16),
             vmem((wrows, width), bf16),
             vmem((wrows, width), f32),
@@ -488,11 +485,11 @@
         ]
         + [dma((2, pairs))] * 4
         + [dma((pairs,))] * 4
-        + [dma, dma((2, nz))]
+        + [dma, dma((2, n // 2))]
         + [dma((n // 2,))] * 3
         + [dma((4, pairs))] * 2
         + [dma((n // 2,))] * 3
-        + [dma((2, nz)), dma, dma, dma((3, pairs)), dma((2,))],
+        + [dma((2, n // 2)), dma, dma, dma((3, pairs)), dma((2,))],
         compiler_params=pltpu.CompilerParams(
             collective_id=0, has_side_effects=True, vmem_limit_bytes=60 * 1024 * 1024
         ),

time: 149 us -> 114 us (0.77)
  the two profiles are of different devices: /device:TPU:28 before, /device:TPU:22 now
where the time goes in v2:
time: 114 us
  Pallas kernels  106 us (93%)
  local copies, waits for them, and re-layouts  6.77 us (6%)
    pallas_call x1, Pallas kernels, layer(): pl.pallas_call(functools.partial(layer_kernel, n, blocks, listed, block,...  106 us
    unnamed x13, local copies, waits for them, and re-layouts  6.77 us

profile of v2, /device:TPU:22, one launch (start us, length us, event | category | flops | bytes accessed | tf_op | source)
XLA Modules:
  0.0 113.6 jit_solution(16007258143719608140)
XLA Ops:
  0.6 106.2 %contact_layer.1 = (bf16[384,1024]{1,0:T(8,128)(2,1)}, bf16[384,1024]{1,0:T(8,128)(2,1)}, bf16[384,1024]{1,0:T(8,128)(2,1)}, bf16[384,1024]{1,0:T(8,128)(2,1)}, f32[64,1024]{1,0:T(8,128)}) custom-call(s32[3,6]{1,0:T(4,128)} %contacts.1, s32[3]{0:T(128)} %count.1, s32[48,128]{1,0:T(8,128)} %bitcast.1, bf16[384,1024]{1,0:T(8,128)(2,1)} %q_hbm.1, ...), custom_call_target="tpu_custom_call" | custom-call | tf_op jit(solution)/shard_map/contact_layer/pallas_call | solution.py:450
  106.8 0.0 copy-start.2
  106.8 2.1 %copy.18 = bf16[384,1024]{1,0:T(8,128)(2,1)} copy(bf16[384,1024]{1,0:T(8,128)(2,1)} %get-tuple-element.10) | data formatting | bytes 1572864
  108.9 0.0 copy-done.2
  109.0 0.0 copy-start.1
  109.0 0.9 copy.19
  109.8 0.5 copy-done.1
  110.4 0.0 copy-start
  110.4 0.9 copy.20
  111.3 0.5 copy-done
  111.8 0.0 copy-start.3
  111.8 0.9 copy.21
  112.7 0.2 copy-done.3
  112.9 0.7 copy.22
Async XLA Ops:
  106.8 2.1 %copy-start.2 = (bf16[384,1024]{1,0:T(8,128)(2,1)S(1)}, bf16[384,1024]{1,0:T(8,128)(2,1)}, u32[]{:S(2)}) copy-start(bf16[384,1024]{1,0:T(8,128)(2,1)} %get-tuple-element.11) | copy-start | bytes 2359300
  109.0 1.4 %copy-start.1 = (bf16[384,1024]{1,0:T(8,128)(2,1)S(1)}, bf16[384,1024]{1,0:T(8,128)(2,1)}, u32[]{:S(2)}) copy-start(bf16[384,1024]{1,0:T(8,128)(2,1)} %get-tuple-element.12) | copy-start | bytes 2359300
  110.4 1.4 %copy-start = (bf16[384,1024]{1,0:T(8,128)(2,1)S(1)}, bf16[384,1024]{1,0:T(8,128)(2,1)}, u32[]{:S(2)}) copy-start(bf16[384,1024]{1,0:T(8,128)(2,1)} %get-tuple-element.13) | copy-start | bytes 2359300
  111.8 1.1 copy-start.3

commit v3 on v2

--- a/solution.py
+++ b/solution.py
@@ -11,8 +11,7 @@
 HEADS = 16
 REACH_DEV = 2
 LANES = 128
-AHEAD_KV = 3
-LEAD = 4
+AHEAD_KV = 5
 
 
 def layer_kernel(
@@ -125,18 +124,23 @@
         zc = chip // 2
         return (z >= zc) & (z + 1 < nz), (z <= zc) & (z > 0)
 
-    def w_hop(p, lead):
-        for i in range(chips):
-            chip = turn(p) * chips + i
-            far_off = jnp.abs(z - chip // 2)
-
-            @pl.when(jnp.maximum(1, LEAD - far_off) == lead)
-            def _(chip=chip):
-                up, down = w_goes(chip)
-                pl.when(chip != mychip)(lambda: w_in(chip).wait_recv())
-                pl.when(up)(lambda: w_z(chip, 1).start())
-                pl.when(down)(lambda: w_z(chip, 0).start())
-                w_c(chip).start()
+    def w_hops(now):
+        def visit(q):
+            for i in range(chips):
+                chip = turn(q) * chips + i
+                far_off = jnp.minimum(jnp.abs(z - chip // 2), 3)
+                late = jnp.where(q < 2, far_off - 3, jnp.where(q < 4, far_off - 2, 2 * far_off - 3))
+                late = jnp.where(q < 6, late, 2 * far_off - 1)
+
+                @pl.when(jnp.where(far_off == 0, -3, late) == now)
+                def _(chip=chip):
+                    up, down = w_goes(chip)
+                    pl.when(chip != mychip)(lambda: w_in(chip).wait_recv())
+                    pl.when(up)(lambda: w_z(chip, 1).start())
+                    pl.when(down)(lambda: w_z(chip, 0).start())
+                    w_c(chip).start()
+
+        over(0, pairs, visit)
 
     def w_wait(p):
         for i in range(chips):
@@ -223,14 +227,14 @@
             zc = chip // 2
             stage = jnp.where(z < zc, z, nz - 1 - z)
 
-            @pl.when((z != zc) & (stage > 0) & (jnp.minimum(stage + 1, LEAD - 1) == lag))
+            @pl.when((z != zc) & (stage > 0) & (2 * jnp.minimum(stage, 2) + 1 == lag))
             def _(chip=chip, zc=zc):
                 side = (z > zc).astype(jnp.int32)
                 gw_in(chip, side).wait_recv()
                 gsum[chip] = (gsum[chip].astype(f32) + gin[side, chip].astype(f32)).astype(bf16)
                 gw_z(chip).start()
 
-            @pl.when((z == zc) & (jnp.minimum(jnp.maximum(zc, nz - 1 - zc) + 1, LEAD) == lag))
+            @pl.when((z == zc) & (2 * jnp.minimum(jnp.maximum(zc, nz - 1 - zc), 3) + 1 == lag))
             def _(chip=chip):
                 yc = lax.rem(chip, 2)
                 pl.when(z > 0)(lambda: gw_in(chip, 0).wait_recv())
@@ -259,8 +263,9 @@
     pl.when(z < nz - 1)(lambda: hello(me + 4))
     pl.semaphore_wait(barrier, 2 + (z > 0).astype(jnp.int32) + (z < nz - 1).astype(jnp.int32))
 
-    w_y().start()
-    kv_start(0)
+    def urgent(p):
+        return mychip // chips == turn(p)
+
     loads = [
         pltpu.make_async_copy(w_hbm, wbuf.at[shard(me)], local_sem.at[0]),
         pltpu.make_async_copy(g_hbm, g_v, local_sem.at[1]),
@@ -268,10 +273,12 @@
         pltpu.make_async_copy(k_hbm, k_v, local_sem.at[3]),
         pltpu.make_async_copy(v_hbm, v_v, local_sem.at[4]),
     ]
-    for copy in loads:
+    loads[0].start()
+    pl.when(urgent(0))(lambda: w_y().start())
+    kv_start(0)
+    pl.when(jnp.logical_not(urgent(0)))(lambda: w_y().start())
+    for copy in loads[1:]:
         copy.start()
-    for p in range(1, AHEAD_KV):
-        kv_start(p)
     loads[0].wait()
 
     first = me * blocks - reach
@@ -308,6 +315,24 @@
         zero = jnp.zeros_like(x)
         return jnp.concatenate([jnp.where(lane, x, zero), jnp.where(lane, zero, x)], axis=0).astype(bf16)
 
+    def among(q, body):
+        pl.when((q >= 0) & (q < pairs))(lambda: body(q))
+
+    def gw_hops(p):
+        for lag in (3, 5, 7):
+            among(p - lag, lambda q, lag=lag: gw_hop(q, lag))
+
+    def serve(p):
+        among(p + AHEAD_KV, kv_start)
+        among(p - 1, ret_two)
+        among(p + 3, kv_first)
+        among(p - 3, ret_three)
+        among(p + 1, kv_second)
+        w_hops(p)
+        among(p - 1, gw_two)
+        gw_hops(p)
+        among(p - 6, ret_four)
+
     def attend(p):
         cols = lanes(p)
         grad_all = lax.dot_general(
@@ -318,6 +343,8 @@
             kwin[span] = (k_v[:, cols] if piece is None else land[p, piece, 0]).reshape(blocks, block, LANES)
             vwin[span] = (v_v[:, cols] if piece is None else land[p, piece, 1]).reshape(blocks, block, LANES)
         for b in range(blocks):
+            if b == blocks - 1:
+                serve(p)
             here = pl.ds(b * block, block)
             for j in range(listed):
                 at = jnp.clip(contacts[b, j] - first, 0, windows - 1)
@@ -368,37 +395,43 @@
         ).astype(bf16)
         gw_one(p)
 
-    def among(q, body):
-        pl.when((q >= 0) & (q < pairs))(lambda: body(q))
-
     def step(p):
-        pl.when((p >= 0) & (p + AHEAD_KV < pairs))(lambda: kv_start(p + AHEAD_KV))
-        among(p + 2, kv_first)
-        among(p + 1, kv_second)
-        for lead in range(LEAD, 0, -1):
-            among(p + lead, lambda q, lead=lead: w_hop(q, lead))
-        pl.when(p == -2)(setup)
-
-        @pl.when((p >= 0) & (p < pairs))
-        def _():
-            kv_wait(p)
-            w_wait(p)
-            attend(p)
-
-        among(p - 1, ret_two)
-        among(p - 1, gw_two)
-        among(p - 2, ret_three)
-
-        @pl.when(p == pairs)
-        def _():
-            mix_v[...] = jnp.dot(att_v[...], wbuf[...], preferred_element_type=f32).astype(bf16)
-            pltpu.make_async_copy(mix_v, mixed_hbm, fin_sem.at[0]).start()
-
-        among(p - 3, ret_four)
-        for lag in range(2, LEAD + 1):
-            among(p - lag, lambda q, lag=lag: gw_hop(q, lag))
-
-    over(-LEAD, pairs + LEAD, step)
+        kv_wait(p)
+        w_wait(p)
+        attend(p)
+
+    w_hops(jnp.int32(-3))
+    for p in range(1, AHEAD_KV):
+        kv_start(p)
+    setup()
+    w_hops(jnp.int32(-2))
+    kv_first(0)
+    w_hops(jnp.int32(-1))
+    kv_first(1)
+    kv_second(0)
+    kv_first(2)
+    over(0, pairs, step)
+    done = jnp.int32(pairs)
+    ret_two(done - 1)
+    ret_three(done - 3)
+    gw_two(done - 1)
+    gw_hops(done)
+    ret_three(done - 2)
+    mix_v[...] = jnp.dot(att_v[...], wbuf[...], preferred_element_type=f32).astype(bf16)
+    pltpu.make_async_copy(mix_v, mixed_hbm, fin_sem.at[0]).start()
+    gw_hops(done + 1)
+    ret_three(done - 1)
+    gw_hops(done + 2)
+    ret_four(done - 6)
+    ret_four(done - 5)
+    gw_hops(done + 3)
+    ret_four(done - 4)
+    gw_hops(done + 4)
+    gw_hops(done + 5)
+    gw_hops(done + 6)
+    ret_four(done - 3)
+    ret_four(done - 2)
+    ret_four(done - 1)
 
     gw_y().wait_recv()
     gwout[...] = (gfin[...] + ybuf[...].astype(f32)) * jnp.float32(1.0 / math.sqrt(tokens))
@@ -497,10 +530,27 @@
     )(contacts, count, ids, queries, keys, values, weight, grad_output)
 
 
+def hand_over_kernel(*refs):
+    for src, dst in zip(refs[: len(refs) // 2], refs[len(refs) // 2 :]):
+        dst[...] = src[...]
+
+
+def hand_over(arrays, parts=2):
+    specs = [pl.BlockSpec((a.shape[0] // parts, a.shape[1]), lambda i: (i, 0)) for a in arrays]
+    return pl.pallas_call(
+        hand_over_kernel,
+        grid=(parts,),
+        in_specs=specs,
+        out_specs=specs,
+        out_shape=[jax.ShapeDtypeStruct(a.shape, a.dtype) for a in arrays],
+        name="hand_over",
+    )(*arrays)
+
+
 def shards(queries, keys, values, out_weight, grad_output, complex_id, contacts, contact_count):
     block = queries.shape[0] // contacts.shape[0]
-    return layer(
-        contacts, contact_count, complex_id.reshape(-1, block), queries, keys, values, out_weight, grad_output
+    return hand_over(
+        layer(contacts, contact_count, complex_id.reshape(-1, block), queries, keys, values, out_weight, grad_output)
     )
 
 

time: 114 us -> 107 us (0.939)
  local copies, waits for them, and re-layouts: 6.77 us -> 0 us
    unnamed x13 -> x0, local copies, waits for them, and re-layouts: 6.77 us -> none
    pallas_call x1, Pallas kernels: 106 us -> 102 us  [layer(): pl.pallas_call(functools.partial(layer_kernel, n, blocks, listed, block,...]
    pallas_call x0 -> x1, Pallas kernels: none -> 3.25 us  [hand_over(): pl.pallas_call(hand_over_kernel, grid=(parts,), in_specs=specs, out_specs...]
where the time goes in v3:
time: 107 us; the launch traced here: 106 us
  Pallas kernels  105 us (98%)
    pallas_call x1, Pallas kernels, layer(): pl.pallas_call(functools.partial(layer_kernel, n, blocks, listed, block,...  102 us
    pallas_call x1, Pallas kernels, hand_over(): pl.pallas_call(hand_over_kernel, grid=(parts,), in_specs=specs, out_specs...  3.25 us

profile of v3, /device:TPU:22, one launch (start us, length us, event | category | flops | bytes accessed | tf_op | source)
XLA Modules:
  0.0 106.0 jit_solution(15168438279499654438)
XLA Ops:
  0.6 102.1 %contact_layer.1 = (bf16[384,1024]{1,0:T(8,128)(2,1)}, bf16[384,1024]{1,0:T(8,128)(2,1)}, bf16[384,1024]{1,0:T(8,128)(2,1)}, bf16[384,1024]{1,0:T(8,128)(2,1)}, f32[64,1024]{1,0:T(8,128)}) custom-call(s32[3,6]{1,0:T(4,128)} %contacts.1, s32[3]{0:T(128)} %count.1, s32[48,128]{1,0:T(8,128)} %bitcast.1, bf16[384,1024]{1,0:T(8,128)(2,1)} %q_hbm.1, ...), custom_call_target="tpu_custom_call" | custom-call | tf_op jit(solution)/shard_map/contact_layer/pallas_call | solution.py:483
  102.7 3.2 %hand_over.1 = (bf16[384,1024]{1,0:T(8,128)(2,1)}, bf16[384,1024]{1,0:T(8,128)(2,1)}, bf16[384,1024]{1,0:T(8,128)(2,1)}, bf16[384,1024]{1,0:T(8,128)(2,1)}, f32[64,1024]{1,0:T(8,128)}) custom-call(bf16[384,1024]{1,0:T(8,128)(2,1)} %get-tuple-element.10.refs_0_, bf16[384,1024]{1,0:T(8,128)(2,1)} %get-tuple-element.11.refs_1_, ...), custom_call_target="tpu_custom_call" | custom-call | tf_op jit(solution)/shard_map/hand_over/pallas_call | solution.py:540

commit v4 on v3

--- a/solution.py
+++ b/solution.py
@@ -124,15 +124,17 @@
         zc = chip // 2
         return (z >= zc) & (z + 1 < nz), (z <= zc) & (z > 0)
 
-    def w_hops(now):
+    def w_hops(now, start=0):
         def visit(q):
             for i in range(chips):
                 chip = turn(q) * chips + i
                 far_off = jnp.minimum(jnp.abs(z - chip // 2), 3)
-                late = jnp.where(q < 2, far_off - 3, jnp.where(q < 4, far_off - 2, 2 * far_off - 3))
+                late = jnp.where(q < 1, jnp.minimum(far_off, 2) - 3, jnp.where(q < 4, far_off - 2, 2 * far_off - 3))
                 late = jnp.where(q < 6, late, 2 * far_off - 1)
-
-                @pl.when(jnp.where(far_off == 0, -3, late) == now)
+                near = jnp.where(q < 1, -3, jnp.where(q < 4, -2, -1))
+                near = jnp.where(chip == mychip, -4, near)
+
+                @pl.when(jnp.where(far_off == 0, near, late) == now)
                 def _(chip=chip):
                     up, down = w_goes(chip)
                     pl.when(chip != mychip)(lambda: w_in(chip).wait_recv())
@@ -140,7 +142,7 @@
                     pl.when(down)(lambda: w_z(chip, 0).start())
                     w_c(chip).start()
 
-        over(0, pairs, visit)
+        over(start, pairs, visit)
 
     def w_wait(p):
         for i in range(chips):
@@ -328,7 +330,7 @@
         among(p + 3, kv_first)
         among(p - 3, ret_three)
         among(p + 1, kv_second)
-        w_hops(p)
+        pl.when(p < 6)(lambda: w_hops(p, 1))
         among(p - 1, gw_two)
         gw_hops(p)
         among(p - 6, ret_four)
@@ -400,14 +402,15 @@
         w_wait(p)
         attend(p)
 
-    w_hops(jnp.int32(-3))
+    w_hops(jnp.int32(-4))
     for p in range(1, AHEAD_KV):
         kv_start(p)
     setup()
+    w_hops(jnp.int32(-3))
+    kv_first(0)
     w_hops(jnp.int32(-2))
-    kv_first(0)
+    kv_first(1)
     w_hops(jnp.int32(-1))
-    kv_first(1)
     kv_second(0)
     kv_first(2)
     over(0, pairs, step)

time: 107 us -> 105 us (0.981)
  Pallas kernels: 105 us -> 103 us
    pallas_call x1, Pallas kernels: 102 us -> 99.7 us  [layer(): pl.pallas_call(functools.partial(layer_kernel, n, blocks, listed, block,...]
where the time goes in v4:
time: 105 us; the launch traced here: 104 us
  Pallas kernels  103 us (98%)
    pallas_call x1, Pallas kernels, layer(): pl.pallas_call(functools.partial(layer_kernel, n, blocks, listed, block,...  99.7 us
    pallas_call x1, Pallas kernels, hand_over(): pl.pallas_call(hand_over_kernel, grid=(parts,), in_specs=specs, out_specs...  3.25 us

profile of v4, /device:TPU:22, one launch (start us, length us, event | category | flops | bytes accessed | tf_op | source)
XLA Modules:
  0.0 103.6 jit_solution(16489398001412971266)
XLA Ops:
  0.6 99.7 %contact_layer.1 = (bf16[384,1024]{1,0:T(8,128)(2,1)}, bf16[384,1024]{1,0:T(8,128)(2,1)}, bf16[384,1024]{1,0:T(8,128)(2,1)}, bf16[384,1024]{1,0:T(8,128)(2,1)}, f32[64,1024]{1,0:T(8,128)}) custom-call(s32[3,6]{1,0:T(4,128)} %contacts.1, s32[3]{0:T(128)} %count.1, s32[48,128]{1,0:T(8,128)} %bitcast.1, bf16[384,1024]{1,0:T(8,128)(2,1)} %q_hbm.1, ...), custom_call_target="tpu_custom_call" | custom-call | tf_op jit(solution)/shard_map/contact_layer/pallas_call | solution.py:486
  100.4 3.2 %hand_over.1 = (bf16[384,1024]{1,0:T(8,128)(2,1)}, bf16[384,1024]{1,0:T(8,128)(2,1)}, bf16[384,1024]{1,0:T(8,128)(2,1)}, bf16[384,1024]{1,0:T(8,128)(2,1)}, f32[64,1024]{1,0:T(8,128)}) custom-call(bf16[384,1024]{1,0:T(8,128)(2,1)} %get-tuple-element.10.refs_0_, bf16[384,1024]{1,0:T(8,128)(2,1)} %get-tuple-element.11.refs_1_, ...), custom_call_target="tpu_custom_call" | custom-call | tf_op jit(solution)/shard_map/hand_over/pallas_call | solution.py:543

commit v5 on v4

--- a/solution.py
+++ b/solution.py
@@ -330,7 +330,7 @@
         among(p + 3, kv_first)
         among(p - 3, ret_three)
         among(p + 1, kv_second)
-        pl.when(p < 6)(lambda: w_hops(p, 1))
+        pl.when((p == 0) | ((p < 6) & (lax.rem(p, 2) == 1)))(lambda: w_hops(p, 1))
         among(p - 1, gw_two)
         gw_hops(p)
         among(p - 6, ret_four)
@@ -533,19 +533,27 @@
     )(contacts, count, ids, queries, keys, values, weight, grad_output)
 
 
-def hand_over_kernel(*refs):
-    for src, dst in zip(refs[: len(refs) // 2], refs[len(refs) // 2 :]):
-        dst[...] = src[...]
-
-
-def hand_over(arrays, parts=2):
-    specs = [pl.BlockSpec((a.shape[0] // parts, a.shape[1]), lambda i: (i, 0)) for a in arrays]
+def hand_over_kernel(count, *refs):
+    held, sems = refs[2 * count : -1], refs[-1]
+    reads = [pltpu.make_async_copy(refs[i], held[i], sems.at[0, i]) for i in range(count)]
+    writes = [pltpu.make_async_copy(held[i], refs[count + i], sems.at[1, i]) for i in range(count)]
+    for copy in reads:
+        copy.start()
+    for read, write in zip(reads, writes):
+        read.wait()
+        write.start()
+    for copy in writes:
+        copy.wait()
+
+
+def hand_over(arrays):
+    hbm = pl.BlockSpec(memory_space=pl.ANY)
     return pl.pallas_call(
-        hand_over_kernel,
-        grid=(parts,),
-        in_specs=specs,
-        out_specs=specs,
+        functools.partial(hand_over_kernel, len(arrays)),
+        in_specs=[hbm] * len(arrays),
+        out_specs=[hbm] * len(arrays),
         out_shape=[jax.ShapeDtypeStruct(a.shape, a.dtype) for a in arrays],
+        scratch_shapes=[pltpu.VMEM(a.shape, a.dtype) for a in arrays] + [pltpu.SemaphoreType.DMA((2, len(arrays)))],
         name="hand_over",
     )(*arrays)
 

time: 105 us -> 105 us (level)
  no operation moved by 1% of the time
where the time goes in v5:
time: 105 us; the launch traced here: 103 us
  Pallas kernels  103 us (98%)
    pallas_call x1, Pallas kernels, layer(): pl.pallas_call(functools.partial(layer_kernel, n, blocks, listed, block,...  99.7 us
    pallas_call x1, Pallas kernels, hand_over(): pl.pallas_call(functools.partial(hand_over_kernel, len(arrays)), in_specs...  2.96 us

profile of v5, /device:TPU:22, one launch (start us, length us, event | category | flops | bytes accessed | tf_op | source)
XLA Modules:
  0.0 103.3 jit_solution(11719181210326811348)
XLA Ops:
  0.6 99.7 %contact_layer.1 = (bf16[384,1024]{1,0:T(8,128)(2,1)}, bf16[384,1024]{1,0:T(8,128)(2,1)}, bf16[384,1024]{1,0:T(8,128)(2,1)}, bf16[384,1024]{1,0:T(8,128)(2,1)}, f32[64,1024]{1,0:T(8,128)}) custom-call(s32[3,6]{1,0:T(4,128)} %contacts.1, s32[3]{0:T(128)} %count.1, s32[48,128]{1,0:T(8,128)} %bitcast.1, bf16[384,1024]{1,0:T(8,128)(2,1)} %q_hbm.1, ...), custom_call_target="tpu_custom_call" | custom-call | tf_op jit(solution)/shard_map/contact_layer/pallas_call | solution.py:486
  100.3 3.0 %hand_over.1 = (bf16[384,1024]{1,0:T(8,128)(2,1)}, bf16[384,1024]{1,0:T(8,128)(2,1)}, bf16[384,1024]{1,0:T(8,128)(2,1)}, bf16[384,1024]{1,0:T(8,128)(2,1)}, f32[64,1024]{1,0:T(8,128)}) custom-call(bf16[384,1024]{1,0:T(8,128)(2,1)} %get-tuple-element.10.refs_0_, bf16[384,1024]{1,0:T(8,128)(2,1)} %get-tuple-element.11.refs_1_, ...), custom_call_target="tpu_custom_call" | custom-call | tf_op jit(solution)/shard_map/hand_over/pallas_call | solution.py:551

commit v6 on v5

--- a/solution.py
+++ b/solution.py
@@ -71,11 +71,11 @@
             (k_hbm, v_hbm)[a].at[:, lanes(p)], land.at[p, 1 + core, a], c_s.at[a, p], c_r.at[a, p], cpeer
         )
 
-    def kv_z(p):
-        return remote(land.at[p, 3 - 3 * y], land.at[p, 3 * y], z_s.at[p], z_r.at[p], ahead)
-
-    def kv_on(p):
-        return remote(land.at[p, 3 - 3 * core], land.at[p, 2 - core], o_s.at[p], o_r.at[p], cpeer)
+    def kv_z(a, p):
+        return remote(land.at[p, 3 - 3 * y, a], land.at[p, 3 * y, a], z_s.at[a, p], z_r.at[a, p], ahead)
+
+    def kv_on(a, p):
+        return remote(land.at[p, 3 - 3 * core, a], land.at[p, 2 - core, a], o_s.at[a, p], o_r.at[a, p], cpeer)
 
     on_sent = (y == core) | has_behind
     on_got = (y != core) | has_behind
@@ -89,19 +89,20 @@
     def kv_first(p):
         for a in range(2):
             kv_y(a, p).wait_recv()
-        pl.when(has_ahead)(lambda: kv_z(p).start())
-        pl.when(y == core)(lambda: kv_on(p).start())
+            pl.when(has_ahead)(lambda a=a: kv_z(a, p).start())
+            pl.when(y == core)(lambda a=a: kv_on(a, p).start())
 
     def kv_second(p):
         @pl.when(has_behind)
         def _():
-            kv_z(p).wait_recv()
-            pl.when(y != core)(lambda: kv_on(p).start())
+            for a in range(2):
+                kv_z(a, p).wait_recv()
+                pl.when(y != core)(lambda a=a: kv_on(a, p).start())
 
     def kv_wait(p):
         for a in range(2):
             kv_c(a, p).wait_recv()
-        pl.when(on_got)(lambda: kv_on(p).wait_recv())
+            pl.when(on_got)(lambda a=a: kv_on(a, p).wait_recv())
 
     mychip = me // 2
 
@@ -446,8 +447,8 @@
         for a in range(2):
             kv_y(a, p).wait_send()
             kv_c(a, p).wait_send()
-        pl.when(has_ahead)(lambda: kv_z(p).wait_send())
-        pl.when(on_sent)(lambda: kv_on(p).wait_send())
+            pl.when(has_ahead)(lambda a=a: kv_z(a, p).wait_send())
+            pl.when(on_sent)(lambda a=a: kv_on(a, p).wait_send())
         pl.when(sent_back)(lambda: back(p).wait_send())
         across(p).wait_send()
         pl.when(has_behind)(lambda: ret_z(p).wait_send())
@@ -519,8 +520,7 @@
             pltpu.SMEM((blocks, 2 * REACH_DEV * blocks + 1), jnp.int32),
             dma((5,)),
         ]
-        + [dma((2, pairs))] * 4
-        + [dma((pairs,))] * 4
+        + [dma((2, pairs))] * 8
         + [dma, dma((2, n // 2))]
         + [dma((n // 2,))] * 3
         + [dma((4, pairs))] * 2

time: 105 us -> 103 us (0.981)
  Pallas kernels: 103 us -> 101 us
    pallas_call x1, Pallas kernels: 99.7 us -> 97.8 us  [layer(): pl.pallas_call(functools.partial(layer_kernel, n, blocks, listed, block,...]
where the time goes in v6:
time: 103 us; the launch traced here: 101 us
  Pallas kernels  101 us (98%)
    pallas_call x1, Pallas kernels, layer(): pl.pallas_call(functools.partial(layer_kernel, n, blocks, listed, block,...  97.8 us
    pallas_call x1, Pallas kernels, hand_over(): pl.pallas_call(functools.partial(hand_over_kernel, len(arrays)), in_specs...  2.96 us

profile of v6, /device:TPU:22, one launch (start us, length us, event | category | flops | bytes accessed | tf_op | source)
XLA Modules:
  0.0 101.4 jit_solution(11149796122930183254)
XLA Ops:
  0.6 97.8 %contact_layer.1 = (bf16[384,1024]{1,0:T(8,128)(2,1)}, bf16[384,1024]{1,0:T(8,128)(2,1)}, bf16[384,1024]{1,0:T(8,128)(2,1)}, bf16[384,1024]{1,0:T(8,128)(2,1)}, f32[64,1024]{1,0:T(8,128)}) custom-call(s32[3,6]{1,0:T(4,128)} %contacts.1, s32[3]{0:T(128)} %count.1, s32[48,128]{1,0:T(8,128)} %bitcast.1, bf16[384,1024]{1,0:T(8,128)(2,1)} %q_hbm.1, ...), custom_call_target="tpu_custom_call" | custom-call | tf_op jit(solution)/shard_map/contact_layer/pallas_call | solution.py:487
  98.5 3.0 %hand_over.1 = (bf16[384,1024]{1,0:T(8,128)(2,1)}, bf16[384,1024]{1,0:T(8,128)(2,1)}, bf16[384,1024]{1,0:T(8,128)(2,1)}, bf16[384,1024]{1,0:T(8,128)(2,1)}, f32[64,1024]{1,0:T(8,128)}) custom-call(bf16[384,1024]{1,0:T(8,128)(2,1)} %get-tuple-element.10.refs_0_, bf16[384,1024]{1,0:T(8,128)(2,1)} %get-tuple-element.11.refs_1_, ...), custom_call_target="tpu_custom_call" | custom-call | tf_op jit(solution)/shard_map/hand_over/pallas_call | solution.py:551
